TPU v7x, 512 devices: a whole 4x8x8 slice. The times are simulated.
512 devices in a mesh: mem: 16 (over z, core), head: 8 (over y), span: 4 (over x).
Axes of the slice: x: 4, y: 8, z: 8, core: 2. Of those that a mesh axis runs over, the one named last changes fastest.
Arguments:
- query: bfloat16 [4, 2048, 8, 8, 128], P('span', 'mem', 'head'), may hold values from -6 to 6
- new_keys: bfloat16 [4, 2048, 8, 128], P('span', 'mem', 'head'), may hold values from -6 to 6
- new_values: bfloat16 [4, 2048, 8, 128], P('span', 'mem', 'head'), may hold values from -5 to 5
- memory_keys: bfloat16 [512, 128, 8, 128], P('mem', None, 'head'), may hold values from -5 to 5
- memory_values: bfloat16 [512, 128, 8, 128], P('mem', None, 'head'), may hold values from -5 to 5
- retrieved: int32 [4, 8, 16], P('span', 'head'), may hold values from 0 to 511, as said below
Outputs:
- attended: bfloat16 [4, 2048, 8192], P('span', ('mem', 'head'))
Inputs may be any that keep to these rules, and one draw needn't show every extreme that they name: Each list retrieved[b, h, :] names 16 different units. The units o * 32 to (o + 1) * 32 - 1 appear at most 3 times in one list, and in every list some o has exactly 3.
All inputs are finite; a program needn't handle non-finite values.
Results may differ from a plain program's by a relative error of at most 0.005.
Values may be sent and summed in bfloat16 or wider, within the bound.
A program may use at most 64 MiB of HBM per device.

v0:
```python
import math

import jax
import jax.numpy as jnp
from jax import lax
from jax.sharding import PartitionSpec as P

NEG = -1e30


def shifted(value, axis, steps):
    count = lax.axis_size(axis)
    first, last = (max(0, -steps), min(count, count - steps))
    return lax.ppermute(value, axis, [(source, source + steps) for source in range(first, last)])


def local(query, new_keys, new_values, memory_keys, memory_values, retrieved):
    queries = query[0]
    row_count, head_count, group_size, head_width = queries.shape
    score_scale = 1.0 / math.sqrt(head_width)
    mem_count = lax.axis_size("mem")
    mem_index = lax.axis_index("mem")
    block_index = lax.axis_index("span")
    row_position = mem_index * row_count + jnp.arange(row_count, dtype=jnp.int32)

    def update(carry_state, key_pair, key_mask):
        old_peak, old_total, old_accum = carry_state
        scores = (
            jnp.einsum("rhgd,khd->rhgk", queries, key_pair[0], preferred_element_type=jnp.float32)
            * score_scale
        )
        scores = jnp.where(key_mask, scores, NEG)
        new_peak = jnp.maximum(old_peak, jnp.max(scores, axis=-1))
        weights = jnp.where(key_mask, jnp.exp(scores - new_peak[..., None]), 0.0)
        factor = jnp.exp(old_peak - new_peak)
        new_total = old_total * factor + jnp.sum(weights, axis=-1)
        new_accum = old_accum * factor[..., None] + jnp.einsum(
            "rhgk,khd->rhgd",
            weights.astype(jnp.bfloat16),
            key_pair[1],
            preferred_element_type=jnp.float32,
        )
        return (new_peak, new_total, new_accum)

    def sweep(carry_state, key_pair, first_key, mask_maker):
        key_count = key_pair.shape[1]
        step_size = math.gcd(key_count, 512)

        def advance(step_index, loop_state):
            sub_pair = lax.dynamic_slice_in_dim(key_pair, step_index * step_size, step_size, 1)
            key_position = (
                first_key + step_index * step_size + jnp.arange(step_size, dtype=jnp.int32)
            )
            return update(loop_state, sub_pair, mask_maker(key_position))

        return lax.fori_loop(0, key_count // step_size, advance, carry_state)

    def current_mask(key_position):
        return (key_position[None, :] <= row_position[:, None])[:, None, None, :]

    def prior_mask(key_position):
        return ((key_position[None, :] > row_position[:, None]) & (block_index > 0))[
            :, None, None, :
        ]

    def full_mask(key_position):
        return jnp.ones((1, 1, 1, key_position.shape[0]), bool)

    carry_state = (
        jnp.full((row_count, head_count, group_size), NEG, jnp.float32),
        jnp.zeros((row_count, head_count, group_size), jnp.float32),
        jnp.zeros((row_count, head_count, group_size, head_width), jnp.float32),
    )
    own_pair = jnp.stack([new_keys[0], new_values[0]])
    prior_pair = shifted(own_pair, "span", 1)
    loop_state = carry_state
    first_key = jnp.int32(0)
    loop_state = sweep(
        loop_state, lax.all_gather(own_pair, "mem", axis=1, tiled=True), first_key, current_mask
    )
    carry_state = sweep(
        loop_state, lax.all_gather(prior_pair, "mem", axis=1, tiled=True), first_key, prior_mask
    )
    unit_lists = retrieved[0]
    list_length = unit_lists.shape[1]
    units_dev = memory_keys.shape[0]
    unit_length = memory_keys.shape[1]
    owners = unit_lists // units_dev
    local_units = unit_lists % units_dev
    owned_here = owners == mem_index
    capacity = max(3, 2 * list_length // mem_count)
    ranking = jnp.cumsum(owned_here.astype(jnp.int32), axis=1) - 1
    slot_range = jnp.arange(capacity, dtype=jnp.int32)
    matches = owned_here[:, :, None] & (ranking[:, :, None] == slot_range[None, None, :])
    picked_units = jnp.sum(jnp.where(matches, local_units[:, :, None], 0), axis=1)
    gathered_pair = []
    for source_array in (memory_keys, memory_values):
        per_head = [source_array[picked_units[0], :, 0, :]]
        gathered_pair.append(jnp.stack(per_head, axis=2))
    block_pair = jnp.stack(gathered_pair).reshape(2, capacity * unit_length, head_count, head_width)
    gathered = lax.all_gather(block_pair, "mem", axis=1, tiled=True)
    gathered = gathered.reshape(2, mem_count * capacity, unit_length, head_count, head_width)
    entry_range = jnp.arange(list_length, dtype=jnp.int32)
    earlier = entry_range[None, :] < entry_range[:, None]
    same_owner = owners[:, :, None] == owners[:, None, :]
    owner_rank = jnp.sum((same_owner & earlier[None, :, :]).astype(jnp.int32), axis=2)
    slot_index = owners * capacity + owner_rank
    live_heads = [gathered[:, :, :, 0, :][:, slot_index[0]]]
    live_pair = jnp.stack(live_heads, axis=3).reshape(
        2, list_length * unit_length, head_count, head_width
    )
    carry_state = sweep(carry_state, live_pair, 0, full_mask)
    final_peak, final_total, final_accum = carry_state
    attended = (final_accum / final_total[..., None]).astype(jnp.bfloat16)
    attended = attended.reshape(row_count, head_count * group_size * head_width)
    moved = lax.all_to_all(attended, "head", split_axis=0, concat_axis=1, tiled=True)
    return moved[None]


def solution(mesh):
    return jax.shard_map(
        local,
        mesh=mesh,
        in_specs=(
            P("span", "mem", "head", None, None),
            P("span", "mem", "head", None),
            P("span", "mem", "head", None),
            P("mem", None, "head", None),
            P("mem", None, "head", None),
            P("span", "head", None),
        ),
        out_specs=P("span", ("mem", "head"), None),
        check_vma=False,
    )
```

profile of v0, /device:TPU:1, one launch (start us, length us, event | category | flops | bytes accessed | tf_op | source)
XLA Modules:
  0.0 191.3 jit_solution(4977924991710813457)
XLA Ops:
  6.5 0.8 constant_dynamic-update-slice_fusion.1
  7.4 0.8 constant_dynamic-update-slice_fusion
  8.2 0.6 copy-done.1
  8.8 3.9 %collective-permute-start = (bf16[2,128,1,128]{3,1,2,0:T(8,128)(2,1)}, bf16[2,128,1,128]{3,1,2,0:T(8,128)(2,1)S(1)}, u32[]{:S(2)}, u32[]{:S(2)}) collective-permute-start(bf16[2,128,1,128]{3,1,2,0:T(8,128)(2,1)} %copy-done.1), channel_id=1, source_target_pairs={{0,1},{1,2},{2,3},{4,5},{5,6},{6,7},{8,9},{9,10},{10,11},{12,13},{... | collective-permute-start | bytes 196616 | tf_op jit(solution)/shard_map/ppermute | solution.py:14
  12.8 1.6 collective-permute-done
  14.4 0.6 copy-done.2
  15.1 0.7 copy.60
  16.0 0.7 and_select_fusion.2
  16.7 0.7 broadcast_compare_fusion.1
  17.4 0.2 fusion.60
  17.5 0.6 gather_fusion
  18.1 1.8 gather_fusion.1
  19.9 0.7 pad_maximum_fusion
  20.7 0.7 fusion.64
  21.3 1.0 copy.81
  22.3 0.2 convert_reduce_fusion
  22.7 34.6 %all-gather.4.cloned.1.call-done = bf16[2,2048,1,128]{3,1,2,0:T(8,128)(2,1)} async-done(((bf16[2,128,1,128]{3,1,2,0:T(8,128)(2,1)}), bf16[2,2048,1,128]{3,1,2,0:T(8,128)(2,1)}) %all-gather.4.cloned.1.call-update) | async-done | bytes 1048592 | tf_op jit(solution)/shard_map/all_gather | solution.py:79
  57.3 18.6 %while.57 = (s32[]{:T(128)}, f32[128,1,8]{0,2,1:T(8,128)S(1)}, f32[128,1,8]{0,2,1:T(8,128)S(1)}, f32[128,1,8,128]{0,3,2,1:T(8,128)}, bf16[2,2048,1,128]{3,1,2,0:...) while((s32[]{:T(128)}, f32[128,1,8]{0,2,1:T(8,128)S(1)}, ...), condition=%wide.region_3.4_spmd.clone, body=%wide.region_0.3_spmd.clone.sunk | while | flops 275716736 | bytes 8197327 | solution.py:56
  57.5 1.4 fusion.89
  58.8 2.4 %fusion.92 = f32[128,1,8,128]{0,3,2,1:T(8,128)} fusion(f32[512,128,8]{1,0,2:T(8,128)S(1)} %get-tuple-element.707, f32[128,8]{0,1:T(8,128)S(1)} %bitcast.263, pred[128,512]{0,1:T(8,128)(4,1)S(1)} %broadcast_compare_fusion.3, f32[128,1,8,128]{0,3,2,1:T(8,128)} %get-tuple-element.724, f32[128,8]{0,1:T(8,128)S(1)} %get-tuple-element.708, ...), kind=kOutput, calls=%fused_computation.61.clone.1 | convolution fusion | flops 137232384 | bytes 3350537 | tf_op jit(solution)/shard_map/while/body/eval_jaxpr/rhgk,khd->rhgd/dot_general | solution.py:37
  61.2 0.5 fusion.91
  61.9 1.4 fusion.89
  63.3 2.6 %fusion.92 = f32[128,1,8,128]{0,3,2,1:T(8,128)} fusion(f32[512,128,8]{1,0,2:T(8,128)S(1)} %get-tuple-element.707, f32[128,8]{0,1:T(8,128)S(1)} %bitcast.263, pred[128,512]{0,1:T(8,128)(4,1)S(1)} %broadcast_compare_fusion.3, f32[128,1,8,128]{0,3,2,1:T(8,128)} %get-tuple-element.724, f32[128,8]{0,1:T(8,128)S(1)} %get-tuple-element.708, ...), kind=kOutput, calls=%fused_computation.61.clone.1 | convolution fusion | flops 137232384 | bytes 3350537 | tf_op jit(solution)/shard_map/while/body/eval_jaxpr/rhgk,khd->rhgd/dot_general | solution.py:37
  65.9 0.5 fusion.91
  66.7 1.4 fusion.89
  68.0 2.6 %fusion.92 = f32[128,1,8,128]{0,3,2,1:T(8,128)} fusion(f32[512,128,8]{1,0,2:T(8,128)S(1)} %get-tuple-element.707, f32[128,8]{0,1:T(8,128)S(1)} %bitcast.263, pred[128,512]{0,1:T(8,128)(4,1)S(1)} %broadcast_compare_fusion.3, f32[128,1,8,128]{0,3,2,1:T(8,128)} %get-tuple-element.724, f32[128,8]{0,1:T(8,128)S(1)} %get-tuple-element.708, ...), kind=kOutput, calls=%fused_computation.61.clone.1 | convolution fusion | flops 137232384 | bytes 3350537 | tf_op jit(solution)/shard_map/while/body/eval_jaxpr/rhgk,khd->rhgd/dot_general | solution.py:37
  70.6 0.5 fusion.91
  71.4 1.4 fusion.89
  72.7 2.6 %fusion.92 = f32[128,1,8,128]{0,3,2,1:T(8,128)} fusion(f32[512,128,8]{1,0,2:T(8,128)S(1)} %get-tuple-element.707, f32[128,8]{0,1:T(8,128)S(1)} %bitcast.263, pred[128,512]{0,1:T(8,128)(4,1)S(1)} %broadcast_compare_fusion.3, f32[128,1,8,128]{0,3,2,1:T(8,128)} %get-tuple-element.724, f32[128,8]{0,1:T(8,128)S(1)} %get-tuple-element.708, ...), kind=kOutput, calls=%fused_computation.61.clone.1 | convolution fusion | flops 137232384 | bytes 3350537 | tf_op jit(solution)/shard_map/while/body/eval_jaxpr/rhgk,khd->rhgd/dot_general | solution.py:37
  75.3 0.5 fusion.91
  75.9 23.7 %all-gather.6.cloned.1.call-done = bf16[2,2048,1,128]{3,1,2,0:T(8,128)(2,1)} async-done(((bf16[2,128,1,128]{3,1,2,0:T(8,128)(2,1)}), bf16[2,2048,1,128]{3,1,2,0:T(8,128)(2,1)}) %all-gather.6.cloned.1.call-update) | async-done | bytes 1048592 | tf_op jit(solution)/shard_map/all_gather | solution.py:82
  99.6 18.8 %while.56 = (s32[]{:T(128)}, f32[128,1,8]{0,2,1:T(8,128)S(1)}, f32[128,1,8]{0,2,1:T(8,128)S(1)}, f32[128,1,8,128]{0,3,2,1:T(8,128)}, pred[]{:T(512)}, /*index=5*...) while((s32[]{:T(128)}, f32[128,1,8]{0,2,1:T(8,128)S(1)}, ...), condition=%wide.region_7.8_spmd.clone, body=%wide.region_4.7_spmd.clone.sunk | while | flops 275648128 | bytes 8197324 | solution.py:56
  99.7 1.4 fusion.84
  101.1 2.6 %fusion.87 = f32[128,1,8,128]{0,3,2,1:T(8,128)} fusion(f32[512,128,8]{1,0,2:T(8,128)S(1)} %get-tuple-element.696, f32[128,8]{0,1:T(8,128)S(1)} %bitcast.261, pred[128,512]{0,1:T(8,128)(4,1)S(1)} %compare_and_fusion.2, f32[128,1,8,128]{0,3,2,1:T(8,128)} %get-tuple-element.761, f32[128,8]{0,1:T(8,128)S(1)} %get-tuple-element.697, ...), kind=kOutput, calls=%fused_computation.32.clone.1 | convolution fusion | flops 137101312 | bytes 3350536 | tf_op jit(solution)/shard_map/while/body/eval_jaxpr/rhgk,khd->rhgd/dot_general | solution.py:37
  103.7 0.5 fusion.86
  104.4 1.4 fusion.84
  105.8 2.6 %fusion.87 = f32[128,1,8,128]{0,3,2,1:T(8,128)} fusion(f32[512,128,8]{1,0,2:T(8,128)S(1)} %get-tuple-element.696, f32[128,8]{0,1:T(8,128)S(1)} %bitcast.261, pred[128,512]{0,1:T(8,128)(4,1)S(1)} %compare_and_fusion.2, f32[128,1,8,128]{0,3,2,1:T(8,128)} %get-tuple-element.761, f32[128,8]{0,1:T(8,128)S(1)} %get-tuple-element.697, ...), kind=kOutput, calls=%fused_computation.32.clone.1 | convolution fusion | flops 137101312 | bytes 3350536 | tf_op jit(solution)/shard_map/while/body/eval_jaxpr/rhgk,khd->rhgd/dot_general | solution.py:37
  108.4 0.5 fusion.86
  109.1 1.4 fusion.84
  110.5 2.6 %fusion.87 = f32[128,1,8,128]{0,3,2,1:T(8,128)} fusion(f32[512,128,8]{1,0,2:T(8,128)S(1)} %get-tuple-element.696, f32[128,8]{0,1:T(8,128)S(1)} %bitcast.261, pred[128,512]{0,1:T(8,128)(4,1)S(1)} %compare_and_fusion.2, f32[128,1,8,128]{0,3,2,1:T(8,128)} %get-tuple-element.761, f32[128,8]{0,1:T(8,128)S(1)} %get-tuple-element.697, ...), kind=kOutput, calls=%fused_computation.32.clone.1 | convolution fusion | flops 137101312 | bytes 3350536 | tf_op jit(solution)/shard_map/while/body/eval_jaxpr/rhgk,khd->rhgd/dot_general | solution.py:37
  113.1 0.5 fusion.86
  113.8 1.4 fusion.84
  115.2 2.6 %fusion.87 = f32[128,1,8,128]{0,3,2,1:T(8,128)} fusion(f32[512,128,8]{1,0,2:T(8,128)S(1)} %get-tuple-element.696, f32[128,8]{0,1:T(8,128)S(1)} %bitcast.261, pred[128,512]{0,1:T(8,128)(4,1)S(1)} %compare_and_fusion.2, f32[128,1,8,128]{0,3,2,1:T(8,128)} %get-tuple-element.761, f32[128,8]{0,1:T(8,128)S(1)} %get-tuple-element.697, ...), kind=kOutput, calls=%fused_computation.32.clone.1 | convolution fusion | flops 137101312 | bytes 3350536 | tf_op jit(solution)/shard_map/while/body/eval_jaxpr/rhgk,khd->rhgd/dot_general | solution.py:37
  117.8 0.5 fusion.86
  118.3 25.6 %all-gather.8.cloned.1.call-done = bf16[2,6144,1,128]{3,1,0,2:T(8,128)(2,1)} async-done(((bf16[2,384,1,128]{3,1,0,2:T(8,128)(2,1)}), bf16[2,6144,1,128]{3,1,0,2:T(8,128)(2,1)}) %all-gather.8.cloned.1.call-update) | async-done | bytes 3145744 | tf_op jit(solution)/shard_map/all_gather | solution.py:101
  143.9 2.6 %gather_fusion.2 = bf16[16,2,128,128]{3,2,1,0:T(8,128)(2,1)S(1)} fusion(bf16[2,48,128,128]{3,2,1,0:T(8,128)(2,1)} %bitcast.269, s32[1024]{0:T(1024)S(1)} %pad_clamp_fusion), kind=kCustom, calls=%fused_computation.2 | custom fusion | bytes 2097216 | tf_op jit(solution)/shard_map/gather | solution.py:108
  146.6 1.1 copy.67
  147.6 17.0 %while.55 = (s32[]{:T(128)}, f32[128,1,8]{0,2,1:T(8,128)S(1)}, f32[128,1,8]{0,2,1:T(8,128)S(1)}, f32[128,1,8,128]{0,3,2,1:T(8,128)}, bf16[2,2048,1,128]{3,1,2,0:...) while((s32[]{:T(128)}, f32[128,1,8]{0,2,1:T(8,128)S(1)}, ...), condition=%wide.region_14.15_spmd, body=%wide.region_11.14_spmd.sunk | while | flops 272894976 | bytes 7930035 | solution.py:56
  147.6 1.3 bitcast_reduce_fusion.2
  149.0 2.5 %fusion.82 = f32[128,1,8,128]{0,3,2,1:T(8,128)} fusion(f32[512,128,8]{1,0,2:T(8,128)S(1)} %get-tuple-element.684, f32[128,8]{0,1:T(8,128)S(1)} %bitcast.259, f32[128,1,8,128]{0,3,2,1:T(8,128)} %get-tuple-element.798, f32[128,8]{0,1:T(8,128)S(1)} %get-tuple-element.685, bf16[2,2048,1,128]{3,1,2,0:T(8,128)(2,1)} %get-tuple-element.810, s32[]{:T(128)S(6)} %add.337, ...), kind=kOutput, calls=%fused_computation.11.clone.1 | convolution fusion | flops 136052736 | bytes 3285000 | tf_op jit(solution)/shard_map/while/body/eval_jaxpr/rhgk,khd->rhgd/dot_general | solution.py:37
  151.5 0.4 fusion.81
  151.9 1.4 bitcast_reduce_fusion.2
  153.2 2.5 %fusion.82 = f32[128,1,8,128]{0,3,2,1:T(8,128)} fusion(f32[512,128,8]{1,0,2:T(8,128)S(1)} %get-tuple-element.684, f32[128,8]{0,1:T(8,128)S(1)} %bitcast.259, f32[128,1,8,128]{0,3,2,1:T(8,128)} %get-tuple-element.798, f32[128,8]{0,1:T(8,128)S(1)} %get-tuple-element.685, bf16[2,2048,1,128]{3,1,2,0:T(8,128)(2,1)} %get-tuple-element.810, s32[]{:T(128)S(6)} %add.337, ...), kind=kOutput, calls=%fused_computation.11.clone.1 | convolution fusion | flops 136052736 | bytes 3285000 | tf_op jit(solution)/shard_map/while/body/eval_jaxpr/rhgk,khd->rhgd/dot_general | solution.py:37
  155.7 0.4 fusion.81
  156.1 1.4 bitcast_reduce_fusion.2
  157.5 2.5 %fusion.82 = f32[128,1,8,128]{0,3,2,1:T(8,128)} fusion(f32[512,128,8]{1,0,2:T(8,128)S(1)} %get-tuple-element.684, f32[128,8]{0,1:T(8,128)S(1)} %bitcast.259, f32[128,1,8,128]{0,3,2,1:T(8,128)} %get-tuple-element.798, f32[128,8]{0,1:T(8,128)S(1)} %get-tuple-element.685, bf16[2,2048,1,128]{3,1,2,0:T(8,128)(2,1)} %get-tuple-element.810, s32[]{:T(128)S(6)} %add.337, ...), kind=kOutput, calls=%fused_computation.11.clone.1 | convolution fusion | flops 136052736 | bytes 3285000 | tf_op jit(solution)/shard_map/while/body/eval_jaxpr/rhgk,khd->rhgd/dot_general | solution.py:37
  159.9 0.4 fusion.81
  160.4 1.4 bitcast_reduce_fusion.2
  161.7 2.5 %fusion.82 = f32[128,1,8,128]{0,3,2,1:T(8,128)} fusion(f32[512,128,8]{1,0,2:T(8,128)S(1)} %get-tuple-element.684, f32[128,8]{0,1:T(8,128)S(1)} %bitcast.259, f32[128,1,8,128]{0,3,2,1:T(8,128)} %get-tuple-element.798, f32[128,8]{0,1:T(8,128)S(1)} %get-tuple-element.685, bf16[2,2048,1,128]{3,1,2,0:T(8,128)(2,1)} %get-tuple-element.810, s32[]{:T(128)S(6)} %add.337, ...), kind=kOutput, calls=%fused_computation.11.clone.1 | convolution fusion | flops 136052736 | bytes 3285000 | tf_op jit(solution)/shard_map/while/body/eval_jaxpr/rhgk,khd->rhgd/dot_general | solution.py:37
  164.2 0.4 fusion.81
  164.6 1.1 divide_convert_fusion
  165.7 0.2 copy.69
  166.0 17.8 %all_to_all.16 = bf16[8,16,1024]{2,1,0:T(8,128)(2,1)S(1)} all-to-all(bf16[8,16,1024]{2,1,0:T(8,128)(2,1)S(1)} %all_to_all.12), channel_id=1, replica_groups=mesh['mem'=16,'head'=8,'span'=4] {'head'}, dimensions={0} | all-to-all | bytes 524288 | tf_op jit(solution)/shard_map/all_to_all | solution.py:116
  184.0 0.8 broadcast_in_dim.170
  (82 shorter events, 2.2 us)
Async XLA Ops:
  6.5 11.0 %copy-start = (bf16[32,128,1,128]{3,1,2,0:T(8,128)(2,1)S(1)}, bf16[32,128,1,128]{3,1,2,0:T(8,128)(2,1)}, u32[]{:S(2)}) copy-start(bf16[32,128,1,128]{3,1,2,0:T(8,128)(2,1)} %param.15) | copy-start | bytes 3145732
  6.5 50.8 %all-gather.4.cloned.1.call-start = ((), (), s32[]{:S(2)}) async-start(), calls=%async_computation.1 | async-start | bytes 1114112 | tf_op jit(solution)/shard_map/all_gather | solution.py:79
  8.2 0.6 copy-start.1
  8.8 90.8 %all-gather.6.cloned.1.call-start = ((), (), s32[]{:S(2)}) async-start(), calls=%async_computation.2 | async-start | bytes 1114112 | tf_op jit(solution)/shard_map/all_gather | solution.py:82
  8.8 5.6 %collective-permute-start = (bf16[2,128,1,128]{3,1,2,0:T(8,128)(2,1)}, bf16[2,128,1,128]{3,1,2,0:T(8,128)(2,1)S(1)}, u32[]{:S(2)}, u32[]{:S(2)}) collective-permute-start(bf16[2,128,1,128]{3,1,2,0:T(8,128)(2,1)} %copy-done.1), channel_id=1, source_target_pairs={{0,1},{1,2},{2,3},{4,5},{5,6},{6,7},{8,9},{9,10},{10,11},{12,13},{... | collective-permute-start | bytes 196616 | tf_op jit(solution)/shard_map/ppermute | solution.py:14
  14.4 0.6 copy-start.2
  15.1 128.9 %all-gather.8.cloned.1.call-start = ((), (), s32[]{:S(2)}) async-start(), calls=%async_computation.3 | async-start | bytes 3342336 | tf_op jit(solution)/shard_map/all_gather | solution.py:101
Sparse Core Ops, SparseCore 0:
  9.5 47.7 all-gather.3
  59.4 40.0 all-gather.5
  101.7 42.1 all-gather.7
where the time goes:
time: 192 us; the launch traced here: 191 us
  waiting for transfers between devices  85.5 us (45%)
  matrix products  46.6 us (24%)
  blocking collectives  17.8 us (9%)
  between operations  13.2 us (7%)
  local copies, waits for them, and re-layouts  12.1 us (6%)
  other arithmetic  11.3 us (6%)
  starting transfers between devices  4.02 us (2%)
    all_gather x1, waiting for transfers between devices, local(): lax.all_gather(own_pair, 'mem', axis=1, tiled=True)  34.6 us
    dot_general x12, matrix products, update(): jnp.einsum('rhgk,khd->rhgd', weights.astype(jnp.bfloat16), key_pair[1], p...  30.3 us
    all_gather x1, waiting for transfers between devices, local(): gathered = lax.all_gather(block_pair, 'mem', axis=1, tiled=True)  25.6 us
    all_gather x1, waiting for transfers between devices, local(): lax.all_gather(prior_pair, 'mem', axis=1, tiled=True)  23.7 us
    all_to_all x1, blocking collectives, local(): lax.all_to_all(attended, 'head', split_axis=0, concat_axis=1, tiled=True)  17.8 us
    dot_general x12, matrix products, update(): jnp.einsum('rhgd,khd->rhgk', queries, key_pair[0], preferred_element_type...  16.3 us
    reduce_sum x12, other arithmetic, update(): new_total = old_total * factor + jnp.sum(weights, axis=-1)  5.5 us
    ppermute x1, starting transfers between devices, shifted(): lax.ppermute(value, axis, [(source, source + steps) for source in range(f...  3.94 us
  transfers between devices with their start and end apart: 4, of which 4 were waited for; matrix products, arithmetic and copies ran while one was open for 23% of the time, Pallas kernels for 0%

commit v1 on v0

v1 whole, which is shorter than its diff:
```python
import functools
import math

import jax
import jax.numpy as jnp
from jax import lax
from jax.experimental import pallas as pl
from jax.experimental.pallas import tpu as pltpu
from jax.sharding import PartitionSpec as P

MESH = pl.DeviceIdType.MESH
NEG = -1e30
LANES = 128
SLOTS = 3
ITEMS = 1 + SLOTS
ROWS = 256


def kernel(
    sizes,
    q_hbm,
    nk_hbm,
    nv_hbm,
    mk_hbm,
    mv_hbm,
    lists,
    o_ref,
    q_v,
    mk_v,
    mv_v,
    buf,
    prev,
    peak,
    accum,
    rows_f32,
    outgoing,
    local_sem,
    recv_sem,
    side_sem,
    up_sem,
    down_sem,
    prev_sem,
    out_send,
    out_recv,
):
    mem_count, head_count, span_count, unit_count, list_length, group, scale = sizes
    ring = mem_count // 2
    steps = ring // 2
    row_count = q_v.shape[0]
    block_rows = row_count // head_count
    mem = lax.axis_index("mem")
    head = lax.axis_index("head")
    span = lax.axis_index("span")
    z = mem // 2
    core = mem % 2

    def device(z_at, core_at, span_at, head_at=None):
        return {
            "mem": lax.rem(z_at + ring, ring) * 2 + core_at,
            "head": head if head_at is None else head_at,
            "span": lax.rem(span_at + span_count, span_count),
        }

    loads = [
        pltpu.make_async_copy(nk_hbm, buf.at[mem, 0, 0], local_sem.at[0]),
        pltpu.make_async_copy(nv_hbm, buf.at[mem, 1, 0], local_sem.at[1]),
        pltpu.make_async_copy(mk_hbm, mk_v, local_sem.at[2]),
        pltpu.make_async_copy(mv_hbm, mv_v, local_sem.at[3]),
        pltpu.make_async_copy(q_hbm, q_v, local_sem.at[4]),
    ]
    for load in loads:
        load.start()

    barrier = pltpu.get_barrier_semaphore()
    near = [
        (dz, 0, dx)
        for dz, dx in ((1, 0), (-1, 0), (0, 1), (0, -1), (1, 1), (-1, -1), (1, -1), (-1, 1))
    ]
    near += [(0, 1, 0), (0, 1, 1), (0, 1, -1)]
    for dz, dc, dx in near:
        pl.semaphore_signal(
            barrier,
            inc=1,
            device_id=device(z + dz, core if dc == 0 else 1 - core, span + dx),
            device_id_type=MESH,
        )
    for dy in range(1, head_count):
        pl.semaphore_signal(
            barrier,
            inc=1,
            device_id=device(z, core, span, lax.rem(head + dy, head_count)),
            device_id_type=MESH,
        )

    def owner(entry):
        return lists[0, entry] // unit_count

    loads[2].wait()
    loads[3].wait()
    picks = [jnp.int32(0)] * SLOTS
    rank = jnp.int32(0)
    for entry in range(list_length):
        here = owner(entry) == mem
        for slot in range(SLOTS):
            picks[slot] = jnp.where(
                here & (rank == slot), lists[0, entry] % unit_count, picks[slot]
            )
        rank = rank + here.astype(jnp.int32)
    for slot in range(SLOTS):
        buf[mem, 0, 1 + slot] = mk_v[picks[slot]]
        buf[mem, 1, 1 + slot] = mv_v[picks[slot]]
    loads[0].wait()
    loads[1].wait()
    loads[4].wait()
    pl.semaphore_wait(barrier, len(near) + head_count - 1)

    def transfer(source, item, send_sem, target):
        return pltpu.make_async_remote_copy(
            src_ref=buf.at[source, :, item],
            dst_ref=buf.at[source, :, item],
            send_sem=send_sem,
            recv_sem=recv_sem.at[source, item],
            device_id=target,
            device_id_type=MESH,
        )

    def send_up(source, item, step):
        shift = jnp.where((z == ring - 1) & (item == 0), 1, 0)
        return transfer(source, item, up_sem.at[step, item], device(z + 1, core, span + shift))

    def send_down(source, item, step):
        first = jnp.where(z > 0, 1, 0)
        later = jnp.where(z > 0, 0, -1)
        shift = jnp.where(item == 0, jnp.where(step == 0, first, later), 0)
        return transfer(source, item, down_sem.at[step, item], device(z - 1, core, span + shift))

    def send_side(source, item):
        own = source == mem
        shift = jnp.where(own & (item == 0), core, 0)
        return transfer(
            source, item, side_sem.at[source // 2, item], device(z, 1 - core, span + shift)
        )

    def send_prev():
        return pltpu.make_async_remote_copy(
            src_ref=buf.at[mem, :, 0],
            dst_ref=prev,
            send_sem=prev_sem.at[0],
            recv_sem=prev_sem.at[1],
            device_id=device(z, core, span + 1),
            device_id_type=MESH,
        )

    send_prev().start()
    for item in range(ITEMS):
        send_up(mem, item, 0).start()
        send_down(mem, item, 0).start()
        send_side(mem, item).start()

    def wait_item(source, item):
        send_side(source, item).wait_recv()

    def slot_bias(source):
        held = jnp.int32(0)
        for entry in range(list_length):
            held = held + (owner(entry) == source).astype(jnp.int32)
        return [
            jnp.full((1, LANES), jnp.where(held > slot, 0.0, NEG), jnp.float32)
            for slot in range(SLOTS)
        ]

    def block_bias(source):
        used = (source < mem) | (span > 0)
        return jnp.full((1, LANES), jnp.where(used, 0.0, NEG), jnp.float32)

    def source_bias(source):
        return jnp.concatenate([block_bias(source)] + slot_bias(source), axis=1)

    def keys_of(source):
        return buf[source, 0].reshape(ITEMS * LANES, LANES)

    def values_of(source):
        return buf[source, 1].reshape(ITEMS * LANES, LANES)

    def attend(start, count, keys, values, bias, fresh):
        rows = pl.ds(pl.multiple_of(start, count), count)
        width = keys.shape[0]
        scores = lax.dot_general(
            q_v[rows, :], keys, (((1,), (1,)), ((), ())), preferred_element_type=jnp.float32
        )
        scores = scores * scale + bias
        best = jnp.max(scores, axis=1, keepdims=True)
        if fresh:
            new_peak = jnp.broadcast_to(best, (count, LANES))
        else:
            old_peak = peak[rows, :]
            new_peak = jnp.maximum(old_peak, best)
        peak[rows, :] = new_peak
        weights = jnp.exp2(scores - jnp.concatenate([new_peak] * (width // LANES), axis=1))
        extended = jnp.concatenate([values, jnp.ones((width, LANES), jnp.bfloat16)], axis=1)
        update = jnp.dot(
            weights.astype(jnp.bfloat16), extended, preferred_element_type=jnp.float32
        )
        if fresh:
            result = update
        else:
            factor = jnp.exp2(old_peak - new_peak)
            result = accum[rows, :] * jnp.concatenate([factor, factor], axis=1) + update
        return rows, result

    send_prev().wait_recv()

    @pl.loop(0, row_count // ROWS)
    def _(block):
        start = block * ROWS
        position = (start + lax.broadcasted_iota(jnp.int32, (ROWS, LANES), 0)) // group
        column = lax.broadcasted_iota(jnp.int32, (ROWS, LANES), 1)
        causal = jnp.where(column <= position, 0.0, NEG)
        after = jnp.where((column > position) & (span > 0), 0.0, NEG)
        wide = [jnp.broadcast_to(b, (ROWS, LANES)) for b in slot_bias(mem)]
        bias = jnp.concatenate([causal] + wide + [after], axis=1)
        keys = jnp.concatenate([keys_of(mem), prev[0]], axis=0)
        values = jnp.concatenate([values_of(mem), prev[1]], axis=0)
        rows, result = attend(start, ROWS, keys, values, bias, True)
        accum[rows, :] = result

    def absorb(source):
        bias = source_bias(source)

        @pl.loop(0, row_count // ROWS)
        def _(block):
            rows, result = attend(
                block * ROWS, ROWS, keys_of(source), values_of(source), bias, False
            )
            accum[rows, :] = result

    def at(z_at, core_at):
        return lax.rem(z_at + ring, ring) * 2 + core_at

    @pl.loop(0, steps * ITEMS)
    def _(tick):
        step = tick // ITEMS + 1
        item = tick % ITEMS
        last = step == steps

        @pl.when(jnp.logical_not(last) | (item < ITEMS // 2))
        def _():
            below = at(z - step, core)
            wait_item(below, item)

            @pl.when((step < steps - 1) | ((step == steps - 1) & (item < ITEMS // 2)))
            def _():
                send_up(below, item, step).start()

            send_side(below, item).start()
            above = at(z + step, core)
            item_down = jnp.where(last, item + ITEMS // 2, item)
            wait_item(above, item_down)

            @pl.when((step < steps - 1) | ((step == steps - 1) & (item >= ITEMS // 2)))
            def _():
                send_down(above, item_down, step).start()

            send_side(above, item_down).start()

        @pl.when((step > 1) | (item == 0))
        def _():
            distance = jnp.where(item % 2 == 0, 1 - step, step - 1)
            other = (item >= ITEMS // 2) | (step == 1)
            source = at(z + distance, jnp.where(other, 1 - core, core))

            @pl.when(other)
            def _():
                for piece in range(ITEMS):
                    wait_item(source, piece)

            absorb(source)

    far = at(z + steps, core)
    far_side = at(z + steps, 1 - core)
    for piece in range(ITEMS):
        wait_item(far_side, piece)

    def send_out(target):
        return pltpu.make_async_remote_copy(
            src_ref=outgoing.at[target],
            dst_ref=o_ref.at[:, pl.ds(pl.multiple_of(head * group * LANES, LANES), group * LANES)],
            send_sem=out_send.at[target],
            recv_sem=out_recv.at[head],
            device_id=device(z, core, span, target),
            device_id_type=MESH,
        )

    def keep_out():
        return pltpu.make_async_copy(
            outgoing.at[head],
            o_ref.at[:, pl.ds(pl.multiple_of(head * group * LANES, LANES), group * LANES)],
            out_send.at[head],
        )

    far_bias = jnp.concatenate([source_bias(far), source_bias(far_side)], axis=1)

    @pl.loop(0, head_count)
    def _(turn):
        half = head_count // 2
        hop = jnp.where(turn % 2 == 0, half + turn // 2, half - (turn + 1) // 2)
        target = lax.rem(head + hop, head_count)
        keys = jnp.concatenate([keys_of(far), keys_of(far_side)], axis=0)
        values = jnp.concatenate([values_of(far), values_of(far_side)], axis=0)
        _, result = attend(target * block_rows, block_rows, keys, values, far_bias, False)
        rows_f32[...] = result[:, :LANES] / result[:, LANES:]
        for member in range(group):
            part = rows_f32[pl.ds(member, block_rows // group, stride=group), :]
            outgoing[target, :, member * LANES : (member + 1) * LANES] = part.astype(jnp.bfloat16)

        @pl.when(target != head)
        def _():
            send_out(target).start()

        @pl.when(target == head)
        def _():
            keep_out().start()

    send_prev().wait_send()

    @pl.loop(0, steps * ITEMS)
    def _(tick):
        step = tick // ITEMS
        item = tick % ITEMS

        @pl.when((step < steps - 1) | (item < ITEMS // 2))
        def _():
            send_up(at(z - step, core), item, step).wait_send()

        @pl.when((step < steps - 1) | (item >= ITEMS // 2))
        def _():
            send_down(at(z + step, core), item, step).wait_send()

    @pl.loop(0, ring * ITEMS)
    def _(tick):
        send_side(at(tick // ITEMS, core), tick % ITEMS).wait_send()

    keep_out().wait()

    @pl.loop(1, head_count)
    def _(hop):
        peer = lax.rem(head + hop, head_count)
        send_out(peer).wait_send()
        pltpu.make_async_remote_copy(
            src_ref=outgoing.at[peer],
            dst_ref=o_ref.at[:, pl.ds(pl.multiple_of(peer * group * LANES, LANES), group * LANES)],
            send_sem=out_send.at[peer],
            recv_sem=out_recv.at[peer],
            device_id=device(z, core, span, peer),
            device_id_type=MESH,
        ).wait_recv()


def local(query, new_keys, new_values, memory_keys, memory_values, retrieved):
    _, length, _, group, width = query.shape
    units, unit_length = memory_keys.shape[0], memory_keys.shape[1]
    mem_count = lax.axis_size("mem")
    head_count = lax.axis_size("head")
    span_count = lax.axis_size("span")
    list_length = retrieved.shape[2]
    ring = mem_count // 2
    steps = ring // 2
    rows = length * group
    scale = math.log2(math.e) / math.sqrt(width)
    sizes = (mem_count, head_count, span_count, units, list_length, group, scale)
    anywhere = pl.BlockSpec(memory_space=pl.ANY)
    dma = pltpu.SemaphoreType.DMA
    out = pl.pallas_call(
        functools.partial(kernel, sizes),
        out_shape=jax.ShapeDtypeStruct(
            (length // head_count, head_count * group * width), jnp.bfloat16
        ),
        in_specs=[anywhere] * 5 + [pl.BlockSpec(memory_space=pltpu.SMEM)],
        out_specs=anywhere,
        scratch_shapes=[
            pltpu.VMEM((rows, width), jnp.bfloat16),
            pltpu.VMEM((units, unit_length, width), jnp.bfloat16),
            pltpu.VMEM((units, unit_length, width), jnp.bfloat16),
            pltpu.VMEM((mem_count, 2, ITEMS, unit_length, width), jnp.bfloat16),
            pltpu.VMEM((2, length, width), jnp.bfloat16),
            pltpu.VMEM((rows, LANES), jnp.float32),
            pltpu.VMEM((rows, 2 * LANES), jnp.float32),
            pltpu.VMEM((rows // head_count, width), jnp.float32),
            pltpu.VMEM((head_count, length // head_count, group * width), jnp.bfloat16),
            dma((5,)),
            dma((mem_count, ITEMS)),
            dma((ring, ITEMS)),
            dma((steps, ITEMS)),
            dma((steps, ITEMS)),
            dma((2,)),
            dma((head_count,)),
            dma((head_count,)),
        ],
        compiler_params=pltpu.CompilerParams(
            collective_id=0, has_side_effects=True, vmem_limit_bytes=62 * 1024 * 1024
        ),
    )(
        query.reshape(rows, width),
        new_keys.reshape(length, width),
        new_values.reshape(length, width),
        memory_keys.reshape(units, unit_length, width),
        memory_values.reshape(units, unit_length, width),
        retrieved.reshape(1, list_length),
    )
    return out[None]


def solution(mesh):
    return jax.shard_map(
        local,
        mesh=mesh,
        in_specs=(
            P("span", "mem", "head", None, None),
            P("span", "mem", "head", None),
            P("span", "mem", "head", None),
            P("mem", None, "head", None),
            P("mem", None, "head", None),
            P("span", "head", None),
        ),
        out_specs=P("span", ("mem", "head"), None),
        check_vma=False,
    )
```

time: 192 us -> 66.3 us (0.35)
  the two profiles are of different devices: /device:TPU:1 before, /device:TPU:2 now
where the time goes in v1:
time: 66.3 us; the launch traced here: 66.1 us
  Pallas kernels  64.5 us (97%)
  local copies, waits for them, and re-layouts  1.67 us (3%)
    pallas_call x1, Pallas kernels, local(): pl.pallas_call(functools.partial(kernel, sizes), out_shape=jax.ShapeDtype...  64.5 us
    unnamed x1, local copies, waits for them, and re-layouts  1.67 us

profile of v1, /device:TPU:2, one launch (start us, length us, event | category | flops | bytes accessed | tf_op | source)
XLA Modules:
  0.0 66.1 jit_solution(16219847424187683844)
XLA Ops:
  0.0 64.5 %shard_map.64 = bf16[16,8192]{1,0:T(8,128)(2,1)} custom-call(bf16[1024,128]{1,0:T(8,128)(2,1)} %bitcast.10, bf16[128,128]{1,0:T(8,128)(2,1)} %bitcast.11, bf16[128,128]{1,0:T(8,128)(2,1)} %bitcast.12, bf16[32,128,128]{2,1,0:T(8,128)(2,1)} %bitcast.8, bf16[32,128,128]{2,1,0:T(8,128)(2,1)} %bitcast.9, s32[1,16]{1,0:T(1,128)} %bitcast.13), custom_call_target="tpu_custom_call" | custom-call | tf_op jit(solution)/shard_map/pallas_call | solution.py:373
  64.5 1.7 %copy.8 = bf16[1,16,8192]{2,1,0:T(8,128)(2,1)} copy(bf16[1,16,8192]{2,1,0:T(8,128)(2,1)} %bitcast.7) | data formatting | bytes 524288

commit v2 on v1

--- a/solution.py
+++ b/solution.py
@@ -9,11 +9,11 @@
 from jax.sharding import PartitionSpec as P
 
 MESH = pl.DeviceIdType.MESH
-NEG = -1e30
 LANES = 128
 SLOTS = 3
 ITEMS = 1 + SLOTS
 ROWS = 256
+HUGE = 1e30
 
 
 def kernel(
@@ -34,6 +34,9 @@
     accum,
     rows_f32,
     outgoing,
+    key_tiles,
+    value_tiles,
+    filler,
     local_sem,
     recv_sem,
     side_sem,
@@ -160,79 +163,95 @@
     def wait_item(source, item):
         send_side(source, item).wait_recv()
 
-    def slot_bias(source):
+    filler[...] = jnp.broadcast_to(buf[mem, 0, 0, 0:1, :], filler.shape)
+
+    def flags_of(source):
         held = jnp.int32(0)
         for entry in range(list_length):
             held = held + (owner(entry) == source).astype(jnp.int32)
-        return [
-            jnp.full((1, LANES), jnp.where(held > slot, 0.0, NEG), jnp.float32)
-            for slot in range(SLOTS)
-        ]
-
-    def block_bias(source):
-        used = (source < mem) | (span > 0)
-        return jnp.full((1, LANES), jnp.where(used, 0.0, NEG), jnp.float32)
-
-    def source_bias(source):
-        return jnp.concatenate([block_bias(source)] + slot_bias(source), axis=1)
-
-    def keys_of(source):
-        return buf[source, 0].reshape(ITEMS * LANES, LANES)
-
-    def values_of(source):
-        return buf[source, 1].reshape(ITEMS * LANES, LANES)
-
-    def attend(start, count, keys, values, bias, fresh):
-        rows = pl.ds(pl.multiple_of(start, count), count)
-        width = keys.shape[0]
+        used = (source < mem) | (span > 0) | (source == mem)
+        return [used] + [held > slot for slot in range(SLOTS)]
+
+    def stage(source, base):
+        for item, flag in enumerate(flags_of(source)):
+            tile = pl.ds((base + item) * LANES, LANES)
+            key_tiles[tile, :] = jnp.where(flag, buf[source, 0, item], filler[...])
+            value_tiles[tile, :LANES] = jnp.where(flag, buf[source, 1, item], jnp.bfloat16(0))
+            value_tiles[tile, LANES:] = jnp.full(
+                (LANES, LANES), jnp.where(flag, 1.0, 0.0), jnp.float32
+            ).astype(jnp.bfloat16)
+
+    def score(rows, width, masks):
         scores = lax.dot_general(
-            q_v[rows, :], keys, (((1,), (1,)), ((), ())), preferred_element_type=jnp.float32
-        )
-        scores = scores * scale + bias
+            q_v[rows, :],
+            key_tiles[:width, :],
+            (((1,), (1,)), ((), ())),
+            preferred_element_type=jnp.float32,
+        )
+        if masks:
+            tiles = [scores[:, t * LANES : (t + 1) * LANES] for t in range(width // LANES)]
+            for t, mask in masks.items():
+                tiles[t] = jnp.where(mask, tiles[t], -HUGE)
+            scores = jnp.concatenate(tiles, axis=1)
+        return scores
+
+    def weigh(rows, width, scores, fresh):
         best = jnp.max(scores, axis=1, keepdims=True)
+        factor = None
         if fresh:
-            new_peak = jnp.broadcast_to(best, (count, LANES))
+            new_peak = jnp.broadcast_to(best, (scores.shape[0], LANES))
         else:
             old_peak = peak[rows, :]
             new_peak = jnp.maximum(old_peak, best)
-        peak[rows, :] = new_peak
-        weights = jnp.exp2(scores - jnp.concatenate([new_peak] * (width // LANES), axis=1))
-        extended = jnp.concatenate([values, jnp.ones((width, LANES), jnp.bfloat16)], axis=1)
-        update = jnp.dot(
-            weights.astype(jnp.bfloat16), extended, preferred_element_type=jnp.float32
-        )
-        if fresh:
-            result = update
-        else:
-            factor = jnp.exp2(old_peak - new_peak)
-            result = accum[rows, :] * jnp.concatenate([factor, factor], axis=1) + update
-        return rows, result
+            factor = jnp.exp2((old_peak - new_peak) * scale)
+        wide_peak = jnp.concatenate([new_peak] * (width // LANES), axis=1)
+        weights = jnp.exp2((scores - wide_peak) * scale)
+        return new_peak, factor, weights.astype(jnp.bfloat16)
+
+    def combine(rows, width, weights, factor):
+        result = jnp.dot(weights, value_tiles[:width, :], preferred_element_type=jnp.float32)
+        if factor is not None:
+            result = accum[rows, :] * jnp.concatenate([factor, factor], axis=1) + result
+        return result
+
+    def attend_all(blocks, width, masks_of, fresh, finish):
+        count = len(blocks)
+        scores = score(blocks[0], width, masks_of(0))
+        weighed = None
+        for index in range(count + 1):
+            following = None
+            if index + 1 < count:
+                following = score(blocks[index + 1], width, masks_of(index + 1))
+            done = weighed
+            if index < count:
+                weighed = weigh(blocks[index], width, scores, fresh)
+            if done is not None:
+                new_peak, factor, weights = done
+                finish(index - 1, new_peak, combine(blocks[index - 1], width, weights, factor))
+            scores = following
 
     send_prev().wait_recv()
-
-    @pl.loop(0, row_count // ROWS)
-    def _(block):
-        start = block * ROWS
-        position = (start + lax.broadcasted_iota(jnp.int32, (ROWS, LANES), 0)) // group
+    stage(mem, 0)
+    own_tile = pl.ds(ITEMS * LANES, LANES)
+    key_tiles[own_tile, :] = prev[0]
+    value_tiles[own_tile, :LANES] = prev[1]
+    value_tiles[own_tile, LANES:] = jnp.ones((LANES, LANES), jnp.bfloat16)
+    blocks = [pl.ds(start, ROWS) for start in range(0, row_count, ROWS)]
+
+    def own_masks(index):
+        position = (index * ROWS + lax.broadcasted_iota(jnp.int32, (ROWS, LANES), 0)) // group
         column = lax.broadcasted_iota(jnp.int32, (ROWS, LANES), 1)
-        causal = jnp.where(column <= position, 0.0, NEG)
-        after = jnp.where((column > position) & (span > 0), 0.0, NEG)
-        wide = [jnp.broadcast_to(b, (ROWS, LANES)) for b in slot_bias(mem)]
-        bias = jnp.concatenate([causal] + wide + [after], axis=1)
-        keys = jnp.concatenate([keys_of(mem), prev[0]], axis=0)
-        values = jnp.concatenate([values_of(mem), prev[1]], axis=0)
-        rows, result = attend(start, ROWS, keys, values, bias, True)
-        accum[rows, :] = result
+        return {0: column <= position, ITEMS: (column > position) & (span > 0)}
+
+    def keep(index, new_peak, result):
+        peak[blocks[index], :] = new_peak
+        accum[blocks[index], :] = result
+
+    attend_all(blocks, (ITEMS + 1) * LANES, own_masks, True, keep)
 
     def absorb(source):
-        bias = source_bias(source)
-
-        @pl.loop(0, row_count // ROWS)
-        def _(block):
-            rows, result = attend(
-                block * ROWS, ROWS, keys_of(source), values_of(source), bias, False
-            )
-            accum[rows, :] = result
+        stage(source, 0)
+        attend_all(blocks, ITEMS * LANES, lambda index: {}, False, keep)
 
     def at(z_at, core_at):
         return lax.rem(z_at + ring, ring) * 2 + core_at
@@ -298,28 +317,30 @@
             out_send.at[head],
         )
 
-    far_bias = jnp.concatenate([source_bias(far), source_bias(far_side)], axis=1)
-
-    @pl.loop(0, head_count)
-    def _(turn):
-        half = head_count // 2
-        hop = jnp.where(turn % 2 == 0, half + turn // 2, half - (turn + 1) // 2)
-        target = lax.rem(head + hop, head_count)
-        keys = jnp.concatenate([keys_of(far), keys_of(far_side)], axis=0)
-        values = jnp.concatenate([values_of(far), values_of(far_side)], axis=0)
-        _, result = attend(target * block_rows, block_rows, keys, values, far_bias, False)
-        rows_f32[...] = result[:, :LANES] / result[:, LANES:]
+    stage(far, 0)
+    stage(far_side, ITEMS)
+    half = head_count // 2
+    hops = [half]
+    for hop in range(1, half):
+        hops += [half - hop, half + hop]
+    hops += [0]
+    targets = [lax.rem(head + hop, head_count) for hop in hops]
+    parts = [
+        pl.ds(pl.multiple_of(target * block_rows, block_rows), block_rows) for target in targets
+    ]
+
+    def hand_over(turn, new_peak, result):
+        target = targets[turn]
+        rows_f32[turn % 2] = result[:, :LANES] / result[:, LANES:]
         for member in range(group):
-            part = rows_f32[pl.ds(member, block_rows // group, stride=group), :]
+            part = rows_f32[turn % 2, pl.ds(member, block_rows // group, stride=group), :]
             outgoing[target, :, member * LANES : (member + 1) * LANES] = part.astype(jnp.bfloat16)
-
-        @pl.when(target != head)
-        def _():
+        if hops[turn] > 0:
             send_out(target).start()
-
-        @pl.when(target == head)
-        def _():
+        else:
             keep_out().start()
+
+    attend_all(parts, 2 * ITEMS * LANES, lambda turn: {}, False, hand_over)
 
     send_prev().wait_send()
 
@@ -385,8 +406,11 @@
             pltpu.VMEM((2, length, width), jnp.bfloat16),
             pltpu.VMEM((rows, LANES), jnp.float32),
             pltpu.VMEM((rows, 2 * LANES), jnp.float32),
-            pltpu.VMEM((rows // head_count, width), jnp.float32),
+            pltpu.VMEM((2, rows // head_count, width), jnp.float32),
             pltpu.VMEM((head_count, length // head_count, group * width), jnp.bfloat16),
+            pltpu.VMEM((2 * ITEMS * unit_length, width), jnp.bfloat16),
+            pltpu.VMEM((2 * ITEMS * unit_length, 2 * width), jnp.bfloat16),
+            pltpu.VMEM((unit_length, width), jnp.bfloat16),
             dma((5,)),
             dma((mem_count, ITEMS)),
             dma((ring, ITEMS)),

time: 66.3 us -> 51.6 us (0.78)
  the two profiles are of different devices: /device:TPU:2 before, /device:TPU:8 now
where the time goes in v2:
time: 51.6 us; the launch traced here: 51.4 us
  Pallas kernels  49.7 us (96%)
  local copies, waits for them, and re-layouts  1.67 us (3%)
    pallas_call x1, Pallas kernels, local(): pl.pallas_call(functools.partial(kernel, sizes), out_shape=jax.ShapeDtype...  49.7 us
    unnamed x1, local copies, waits for them, and re-layouts  1.67 us

profile of v2, /device:TPU:8, one launch (start us, length us, event | category | flops | bytes accessed | tf_op | source)
XLA Modules:
  0.0 51.4 jit_solution(11767501248172484202)
XLA Ops:
  0.0 49.7 %shard_map.64 = bf16[16,8192]{1,0:T(8,128)(2,1)} custom-call(bf16[1024,128]{1,0:T(8,128)(2,1)} %bitcast.10, bf16[128,128]{1,0:T(8,128)(2,1)} %bitcast.11, bf16[128,128]{1,0:T(8,128)(2,1)} %bitcast.12, bf16[32,128,128]{2,1,0:T(8,128)(2,1)} %bitcast.8, bf16[32,128,128]{2,1,0:T(8,128)(2,1)} %bitcast.9, s32[1,16]{1,0:T(1,128)} %bitcast.13), custom_call_target="tpu_custom_call" | custom-call | tf_op jit(solution)/shard_map/pallas_call | solution.py:394
  49.7 1.7 %copy.8 = bf16[1,16,8192]{2,1,0:T(8,128)(2,1)} copy(bf16[1,16,8192]{2,1,0:T(8,128)(2,1)} %bitcast.7) | data formatting | bytes 524288

commit v3 on v2

--- a/solution.py
+++ b/solution.py
@@ -29,6 +29,7 @@
     mk_v,
     mv_v,
     buf,
+    far,
     prev,
     peak,
     accum,
@@ -37,9 +38,12 @@
     key_tiles,
     value_tiles,
     filler,
+    table,
     local_sem,
     recv_sem,
+    far_sem,
     side_sem,
+    far_side_sem,
     up_sem,
     down_sem,
     prev_sem,
@@ -98,50 +102,52 @@
     def owner(entry):
         return lists[0, entry] // unit_count
 
-    loads[2].wait()
-    loads[3].wait()
-    picks = [jnp.int32(0)] * SLOTS
-    rank = jnp.int32(0)
-    for entry in range(list_length):
-        here = owner(entry) == mem
-        for slot in range(SLOTS):
-            picks[slot] = jnp.where(
-                here & (rank == slot), lists[0, entry] % unit_count, picks[slot]
-            )
-        rank = rank + here.astype(jnp.int32)
-    for slot in range(SLOTS):
-        buf[mem, 0, 1 + slot] = mk_v[picks[slot]]
-        buf[mem, 1, 1 + slot] = mv_v[picks[slot]]
-    loads[0].wait()
-    loads[1].wait()
-    loads[4].wait()
-    pl.semaphore_wait(barrier, len(near) + head_count - 1)
-
-    def transfer(source, item, send_sem, target):
+    def at(z_at, core_at):
+        return lax.rem(z_at + ring, ring) * 2 + core_at
+
+    far_z = lax.rem(z + steps, ring)
+
+    def transfer(source, item, send_sem, target, last=False):
+        if last:
+            landing, landed = far.at[core, :, item], far_sem.at[core, item]
+        else:
+            landing, landed = buf.at[source, :, item], recv_sem.at[source, item]
         return pltpu.make_async_remote_copy(
             src_ref=buf.at[source, :, item],
-            dst_ref=buf.at[source, :, item],
+            dst_ref=landing,
             send_sem=send_sem,
-            recv_sem=recv_sem.at[source, item],
+            recv_sem=landed,
             device_id=target,
             device_id_type=MESH,
         )
 
-    def send_up(source, item, step):
+    def send_up(source, item, step, last=False):
         shift = jnp.where((z == ring - 1) & (item == 0), 1, 0)
-        return transfer(source, item, up_sem.at[step, item], device(z + 1, core, span + shift))
-
-    def send_down(source, item, step):
+        target = device(z + 1, core, span + shift)
+        return transfer(source, item, up_sem.at[step, item], target, last)
+
+    def send_down(source, item, step, last=False):
         first = jnp.where(z > 0, 1, 0)
         later = jnp.where(z > 0, 0, -1)
         shift = jnp.where(item == 0, jnp.where(step == 0, first, later), 0)
-        return transfer(source, item, down_sem.at[step, item], device(z - 1, core, span + shift))
+        target = device(z - 1, core, span + shift)
+        return transfer(source, item, down_sem.at[step, item], target, last)
 
     def send_side(source, item):
         own = source == mem
         shift = jnp.where(own & (item == 0), core, 0)
         return transfer(
             source, item, side_sem.at[source // 2, item], device(z, 1 - core, span + shift)
+        )
+
+    def far_copy(origin, item):
+        return pltpu.make_async_remote_copy(
+            src_ref=far.at[origin, :, item],
+            dst_ref=far.at[origin, :, item],
+            send_sem=far_side_sem.at[item],
+            recv_sem=far_sem.at[origin, item],
+            device_id=device(z, 1 - core, span),
+            device_id_type=MESH,
         )
 
     def send_prev():
@@ -154,32 +160,89 @@
             device_id_type=MESH,
         )
 
-    send_prev().start()
-    for item in range(ITEMS):
+    def wait_item(source, item):
+        send_side(source, item).wait_recv()
+
+    def send_own(item):
         send_up(mem, item, 0).start()
         send_down(mem, item, 0).start()
         send_side(mem, item).start()
 
-    def wait_item(source, item):
-        send_side(source, item).wait_recv()
-
+    loads[0].wait()
+    loads[1].wait()
+    pl.semaphore_wait(barrier, len(near) + head_count - 1)
+    send_own(0)
+    send_prev().start()
+
+    owners = [owner(entry) for entry in range(list_length)]
+    picks = [jnp.int32(0)] * SLOTS
+    rank = jnp.int32(0)
+    for entry in range(list_length):
+        here = owners[entry] == mem
+        for slot in range(SLOTS):
+            picks[slot] = jnp.where(
+                here & (rank == slot), lists[0, entry] % unit_count, picks[slot]
+            )
+        rank = rank + here.astype(jnp.int32)
+    loads[2].wait()
+    loads[3].wait()
+    for slot in range(SLOTS):
+        buf[mem, 0, 1 + slot] = mk_v[picks[slot]]
+        buf[mem, 1, 1 + slot] = mv_v[picks[slot]]
     filler[...] = jnp.broadcast_to(buf[mem, 0, 0, 0:1, :], filler.shape)
 
-    def flags_of(source):
-        held = jnp.int32(0)
+    ranks = []
+    for entry in range(list_length):
+        same = jnp.int32(0)
+        for earlier in range(entry):
+            same = same + (owners[earlier] == owners[entry]).astype(jnp.int32)
+        ranks.append(same)
+    for item in range(1, ITEMS):
+        send_own(item)
+    distant = [(held // 2 == far_z).astype(jnp.int32) for held in owners]
+    place_far = jnp.int32(list_length) - sum(distant)
+    place_near = jnp.int32(0)
+    places = []
+    for entry in range(list_length):
+        places.append(jnp.where(distant[entry] == 1, place_far, place_near))
+        place_far = place_far + distant[entry]
+        place_near = place_near + 1 - distant[entry]
+    for place in range(list_length):
+        code = jnp.int32(0)
         for entry in range(list_length):
-            held = held + (owner(entry) == source).astype(jnp.int32)
-        used = (source < mem) | (span > 0) | (source == mem)
-        return [used] + [held > slot for slot in range(SLOTS)]
-
-    def stage(source, base):
-        for item, flag in enumerate(flags_of(source)):
-            tile = pl.ds((base + item) * LANES, LANES)
-            key_tiles[tile, :] = jnp.where(flag, buf[source, 0, item], filler[...])
-            value_tiles[tile, :LANES] = jnp.where(flag, buf[source, 1, item], jnp.bfloat16(0))
-            value_tiles[tile, LANES:] = jnp.full(
-                (LANES, LANES), jnp.where(flag, 1.0, 0.0), jnp.float32
-            ).astype(jnp.bfloat16)
+            value = owners[entry] * ITEMS + 1 + ranks[entry]
+            code = code + jnp.where(places[entry] == place, value, 0)
+        table[place] = code
+    loads[4].wait()
+
+    def put(tile, keys, values, ones):
+        tile = pl.ds(tile * LANES, LANES)
+        key_tiles[tile, :] = keys
+        value_tiles[tile, :LANES] = values
+        value_tiles[tile, LANES:] = ones
+
+    ones = jnp.ones((LANES, LANES), jnp.bfloat16)
+
+    def put_chunk(tile, source, keys, values):
+        used = (source < mem) | (span > 0)
+        weight = jnp.full((LANES, LANES), jnp.where(used, 1.0, 0.0), jnp.float32)
+        put(
+            tile,
+            jnp.where(used, keys, filler[...]),
+            jnp.where(used, values, jnp.bfloat16(0)),
+            weight.astype(jnp.bfloat16),
+        )
+
+    def put_unit(tile, place, maybe_far):
+        held = table[place] // ITEMS
+        item = table[place] % ITEMS
+        pair = [buf[held, kind, item] for kind in range(2)]
+        if maybe_far:
+            there = held // 2 == far_z
+            pair = [
+                jnp.where(there, far[held % 2, kind, item], pair[kind]) for kind in range(2)
+            ]
+        put(tile, pair[0], pair[1], ones)
 
     def score(rows, width, masks):
         scores = lax.dot_general(
@@ -230,75 +293,91 @@
                 finish(index - 1, new_peak, combine(blocks[index - 1], width, weights, factor))
             scores = following
 
+    put(0, buf[mem, 0, 0], buf[mem, 1, 0], ones)
+    beside = at(z, 1 - core)
+    wait_item(beside, 0)
+    put_chunk(1, beside, buf[beside, 0, 0], buf[beside, 1, 0])
     send_prev().wait_recv()
-    stage(mem, 0)
-    own_tile = pl.ds(ITEMS * LANES, LANES)
-    key_tiles[own_tile, :] = prev[0]
-    value_tiles[own_tile, :LANES] = prev[1]
-    value_tiles[own_tile, LANES:] = jnp.ones((LANES, LANES), jnp.bfloat16)
+    put(2, prev[0], prev[1], ones)
     blocks = [pl.ds(start, ROWS) for start in range(0, row_count, ROWS)]
 
     def own_masks(index):
         position = (index * ROWS + lax.broadcasted_iota(jnp.int32, (ROWS, LANES), 0)) // group
         column = lax.broadcasted_iota(jnp.int32, (ROWS, LANES), 1)
-        return {0: column <= position, ITEMS: (column > position) & (span > 0)}
+        return {0: column <= position, 2: (column > position) & (span > 0)}
 
     def keep(index, new_peak, result):
         peak[blocks[index], :] = new_peak
         accum[blocks[index], :] = result
 
-    attend_all(blocks, (ITEMS + 1) * LANES, own_masks, True, keep)
-
-    def absorb(source):
-        stage(source, 0)
-        attend_all(blocks, ITEMS * LANES, lambda index: {}, False, keep)
-
-    def at(z_at, core_at):
-        return lax.rem(z_at + ring, ring) * 2 + core_at
-
-    @pl.loop(0, steps * ITEMS)
+    attend_all(blocks, 3 * LANES, own_masks, True, keep)
+
+    def absorb(tiles):
+        attend_all(blocks, tiles * LANES, lambda index: {}, False, keep)
+
+    @pl.loop(0, (steps - 1) * ITEMS)
     def _(tick):
         step = tick // ITEMS + 1
         item = tick % ITEMS
-        last = step == steps
-
-        @pl.when(jnp.logical_not(last) | (item < ITEMS // 2))
+        turning = step == steps - 1
+        below = at(z - step, core)
+        wait_item(below, item)
+
+        @pl.when(jnp.logical_not(turning))
         def _():
-            below = at(z - step, core)
-            wait_item(below, item)
-
-            @pl.when((step < steps - 1) | ((step == steps - 1) & (item < ITEMS // 2)))
-            def _():
-                send_up(below, item, step).start()
-
-            send_side(below, item).start()
-            above = at(z + step, core)
-            item_down = jnp.where(last, item + ITEMS // 2, item)
-            wait_item(above, item_down)
-
-            @pl.when((step < steps - 1) | ((step == steps - 1) & (item >= ITEMS // 2)))
-            def _():
-                send_down(above, item_down, step).start()
-
-            send_side(above, item_down).start()
-
-        @pl.when((step > 1) | (item == 0))
+            send_up(below, item, step).start()
+
+        @pl.when(turning & (item < ITEMS // 2))
         def _():
-            distance = jnp.where(item % 2 == 0, 1 - step, step - 1)
-            other = (item >= ITEMS // 2) | (step == 1)
-            source = at(z + distance, jnp.where(other, 1 - core, core))
-
-            @pl.when(other)
-            def _():
-                for piece in range(ITEMS):
-                    wait_item(source, piece)
-
-            absorb(source)
-
-    far = at(z + steps, core)
-    far_side = at(z + steps, 1 - core)
-    for piece in range(ITEMS):
-        wait_item(far_side, piece)
+            send_up(below, item, step, True).start()
+
+        send_side(below, item).start()
+        above = at(z + step, core)
+        wait_item(above, item)
+
+        @pl.when(jnp.logical_not(turning))
+        def _():
+            send_down(above, item, step).start()
+
+        @pl.when(turning & (item >= ITEMS // 2))
+        def _():
+            send_down(above, item, step, True).start()
+
+        send_side(above, item).start()
+
+        @pl.when(item == 1)
+        def _():
+            for tile, (distance, core_at) in enumerate(
+                ((-step, core), (step, core), (-step, 1 - core), (step, 1 - core))
+            ):
+                source = at(z + distance, core_at)
+                if tile >= 2:
+                    wait_item(source, 0)
+                put_chunk(tile, source, buf[source, 0, 0], buf[source, 1, 0])
+            absorb(4)
+
+    early = min(list_length // 2, list_length - 2 * SLOTS)
+    for item in range(1, ITEMS):
+        wait_item(beside, item)
+
+    @pl.loop(0, (steps - 1) * (ITEMS - 1))
+    def _(tick):
+        step = tick // (ITEMS - 1) + 1
+        item = tick % (ITEMS - 1) + 1
+        wait_item(at(z - step, 1 - core), item)
+        wait_item(at(z + step, 1 - core), item)
+
+    for half in range(2):
+        for item in (half, half + ITEMS // 2):
+            far_copy(core, item).wait_recv()
+            far_copy(core, item).start()
+        first, past = half * early // 2, (half + 1) * early // 2
+        for place in range(first, past):
+            put_unit(place - first, place, False)
+        absorb(past - first)
+
+    for item in range(ITEMS):
+        far_copy(1 - core, item).wait_recv()
 
     def send_out(target):
         return pltpu.make_async_remote_copy(
@@ -317,8 +396,10 @@
             out_send.at[head],
         )
 
-    stage(far, 0)
-    stage(far_side, ITEMS)
+    for origin in range(2):
+        put_chunk(origin, far_z * 2 + origin, far[origin, 0, 0], far[origin, 1, 0])
+    for place in range(early, list_length):
+        put_unit(2 + place - early, place, True)
     half = head_count // 2
     hops = [half]
     for hop in range(1, half):
@@ -340,26 +421,31 @@
         else:
             keep_out().start()
 
-    attend_all(parts, 2 * ITEMS * LANES, lambda turn: {}, False, hand_over)
+    attend_all(parts, (2 + list_length - early) * LANES, lambda turn: {}, False, hand_over)
 
     send_prev().wait_send()
 
-    @pl.loop(0, steps * ITEMS)
+    @pl.loop(0, (steps - 1) * ITEMS)
     def _(tick):
         step = tick // ITEMS
         item = tick % ITEMS
-
-        @pl.when((step < steps - 1) | (item < ITEMS // 2))
+        send_up(at(z - step, core), item, step).wait_send()
+        send_down(at(z + step, core), item, step).wait_send()
+        send_side(at(z - step, core), item).wait_send()
+
+        @pl.when(step > 0)
         def _():
-            send_up(at(z - step, core), item, step).wait_send()
-
-        @pl.when((step < steps - 1) | (item >= ITEMS // 2))
-        def _():
-            send_down(at(z + step, core), item, step).wait_send()
-
-    @pl.loop(0, ring * ITEMS)
-    def _(tick):
-        send_side(at(tick // ITEMS, core), tick % ITEMS).wait_send()
+            send_side(at(z + step, core), item).wait_send()
+
+    for item in range(ITEMS // 2):
+        send_up(at(z - steps + 1, core), item, steps - 1, True).wait_send()
+        send_down(at(z + steps - 1, core), item + ITEMS // 2, steps - 1, True).wait_send()
+
+    @pl.loop(0, ITEMS)
+    def _(item):
+        for step in (1 - steps, steps - 1):
+            send_side(at(z + step, core), item).wait_send()
+        far_copy(core, item).wait_send()
 
     keep_out().wait()
 
@@ -387,6 +473,7 @@
     ring = mem_count // 2
     steps = ring // 2
     rows = length * group
+    tiles = 2 + max(list_length, 2 * SLOTS)
     scale = math.log2(math.e) / math.sqrt(width)
     sizes = (mem_count, head_count, span_count, units, list_length, group, scale)
     anywhere = pl.BlockSpec(memory_space=pl.ANY)
@@ -403,17 +490,21 @@
             pltpu.VMEM((units, unit_length, width), jnp.bfloat16),
             pltpu.VMEM((units, unit_length, width), jnp.bfloat16),
             pltpu.VMEM((mem_count, 2, ITEMS, unit_length, width), jnp.bfloat16),
+            pltpu.VMEM((2, 2, ITEMS, unit_length, width), jnp.bfloat16),
             pltpu.VMEM((2, length, width), jnp.bfloat16),
             pltpu.VMEM((rows, LANES), jnp.float32),
             pltpu.VMEM((rows, 2 * LANES), jnp.float32),
             pltpu.VMEM((2, rows // head_count, width), jnp.float32),
             pltpu.VMEM((head_count, length // head_count, group * width), jnp.bfloat16),
-            pltpu.VMEM((2 * ITEMS * unit_length, width), jnp.bfloat16),
-            pltpu.VMEM((2 * ITEMS * unit_length, 2 * width), jnp.bfloat16),
+            pltpu.VMEM((tiles * unit_length, width), jnp.bfloat16),
+            pltpu.VMEM((tiles * unit_length, 2 * width), jnp.bfloat16),
             pltpu.VMEM((unit_length, width), jnp.bfloat16),
+            pltpu.SMEM((list_length,), jnp.int32),
             dma((5,)),
             dma((mem_count, ITEMS)),
+            dma((2, ITEMS)),
             dma((ring, ITEMS)),
+            dma((ITEMS,)),
             dma((steps, ITEMS)),
             dma((steps, ITEMS)),
             dma((2,)),

time: 51.6 us -> 52.4 us (1.016)
  the two profiles are of different devices: /device:TPU:8 before, /device:TPU:1 now
where the time goes in v3:
time: 52.4 us; the launch traced here: 52.2 us
  Pallas kernels  50.5 us (96%)
  local copies, waits for them, and re-layouts  1.67 us (3%)
    pallas_call x1, Pallas kernels, local(): pl.pallas_call(functools.partial(kernel, sizes), out_shape=jax.ShapeDtype...  50.5 us
    unnamed x1, local copies, waits for them, and re-layouts  1.67 us

profile of v3, /device:TPU:1, one launch (start us, length us, event | category | flops | bytes accessed | tf_op | source)
XLA Modules:
  0.0 52.2 jit_solution(4345307081920399911)
XLA Ops:
  0.0 50.5 %shard_map.64 = bf16[16,8192]{1,0:T(8,128)(2,1)} custom-call(bf16[1024,128]{1,0:T(8,128)(2,1)} %bitcast.10, bf16[128,128]{1,0:T(8,128)(2,1)} %bitcast.11, bf16[128,128]{1,0:T(8,128)(2,1)} %bitcast.12, bf16[32,128,128]{2,1,0:T(8,128)(2,1)} %bitcast.8, bf16[32,128,128]{2,1,0:T(8,128)(2,1)} %bitcast.9, s32[1,16]{1,0:T(1,128)} %bitcast.13), custom_call_target="tpu_custom_call" | custom-call | tf_op jit(solution)/shard_map/pallas_call | solution.py:481
  50.5 1.7 %copy.8 = bf16[1,16,8192]{2,1,0:T(8,128)(2,1)} copy(bf16[1,16,8192]{2,1,0:T(8,128)(2,1)} %bitcast.7) | data formatting | bytes 524288

commit v4 on v3

--- a/solution.py
+++ b/solution.py
@@ -75,8 +75,8 @@
         pltpu.make_async_copy(mv_hbm, mv_v, local_sem.at[3]),
         pltpu.make_async_copy(q_hbm, q_v, local_sem.at[4]),
     ]
-    for load in loads:
-        load.start()
+    loads[0].start()
+    loads[1].start()
 
     barrier = pltpu.get_barrier_semaphore()
     near = [
@@ -91,6 +91,8 @@
             device_id=device(z + dz, core if dc == 0 else 1 - core, span + dx),
             device_id_type=MESH,
         )
+    for load in loads[2:]:
+        load.start()
     for dy in range(1, head_count):
         pl.semaphore_signal(
             barrier,
@@ -168,12 +170,6 @@
         send_down(mem, item, 0).start()
         send_side(mem, item).start()
 
-    loads[0].wait()
-    loads[1].wait()
-    pl.semaphore_wait(barrier, len(near) + head_count - 1)
-    send_own(0)
-    send_prev().start()
-
     owners = [owner(entry) for entry in range(list_length)]
     picks = [jnp.int32(0)] * SLOTS
     rank = jnp.int32(0)
@@ -184,6 +180,11 @@
                 here & (rank == slot), lists[0, entry] % unit_count, picks[slot]
             )
         rank = rank + here.astype(jnp.int32)
+    loads[0].wait()
+    loads[1].wait()
+    pl.semaphore_wait(barrier, len(near) + head_count - 1)
+    send_own(0)
+    send_prev().start()
     loads[2].wait()
     loads[3].wait()
     for slot in range(SLOTS):
@@ -293,12 +294,6 @@
                 finish(index - 1, new_peak, combine(blocks[index - 1], width, weights, factor))
             scores = following
 
-    put(0, buf[mem, 0, 0], buf[mem, 1, 0], ones)
-    beside = at(z, 1 - core)
-    wait_item(beside, 0)
-    put_chunk(1, beside, buf[beside, 0, 0], buf[beside, 1, 0])
-    send_prev().wait_recv()
-    put(2, prev[0], prev[1], ones)
     blocks = [pl.ds(start, ROWS) for start in range(0, row_count, ROWS)]
 
     def own_masks(index):
@@ -310,7 +305,15 @@
         peak[blocks[index], :] = new_peak
         accum[blocks[index], :] = result
 
-    attend_all(blocks, 3 * LANES, own_masks, True, keep)
+    beside = at(z, 1 - core)
+
+    def begin():
+        put(0, buf[mem, 0, 0], buf[mem, 1, 0], ones)
+        wait_item(beside, 0)
+        put_chunk(1, beside, buf[beside, 0, 0], buf[beside, 1, 0])
+        send_prev().wait_recv()
+        put(2, prev[0], prev[1], ones)
+        attend_all(blocks, 3 * LANES, own_masks, True, keep)
 
     def absorb(tiles):
         attend_all(blocks, tiles * LANES, lambda index: {}, False, keep)
@@ -345,10 +348,15 @@
 
         send_side(above, item).start()
 
-        @pl.when(item == 1)
-        def _():
+        @pl.when(tick == 1)
+        def _():
+            begin()
+
+        @pl.when((tick > 1) & (tick % 3 == 0))
+        def _():
+            reach = tick // 3
             for tile, (distance, core_at) in enumerate(
-                ((-step, core), (step, core), (-step, 1 - core), (step, 1 - core))
+                ((-reach, core), (reach, core), (-reach, 1 - core), (reach, 1 - core))
             ):
                 source = at(z + distance, core_at)
                 if tile >= 2:

time: 52.4 us -> 52.6 us (level)
  no operation moved by 1% of the time
where the time goes in v4:
time: 52.6 us; the launch traced here: 52.4 us
  Pallas kernels  50.7 us (96%)
  local copies, waits for them, and re-layouts  1.67 us (3%)
    pallas_call x1, Pallas kernels, local(): pl.pallas_call(functools.partial(kernel, sizes), out_shape=jax.ShapeDtype...  50.7 us
    unnamed x1, local copies, waits for them, and re-layouts  1.67 us

profile of v4, /device:TPU:1, one launch (start us, length us, event | category | flops | bytes accessed | tf_op | source)
XLA Modules:
  0.0 52.4 jit_solution(1717598388054297291)
XLA Ops:
  0.0 50.7 %shard_map.64 = bf16[16,8192]{1,0:T(8,128)(2,1)} custom-call(bf16[1024,128]{1,0:T(8,128)(2,1)} %bitcast.10, bf16[128,128]{1,0:T(8,128)(2,1)} %bitcast.11, bf16[128,128]{1,0:T(8,128)(2,1)} %bitcast.12, bf16[32,128,128]{2,1,0:T(8,128)(2,1)} %bitcast.8, bf16[32,128,128]{2,1,0:T(8,128)(2,1)} %bitcast.9, s32[1,16]{1,0:T(1,128)} %bitcast.13), custom_call_target="tpu_custom_call" | custom-call | tf_op jit(solution)/shard_map/pallas_call | solution.py:489
  50.7 1.7 %copy.8 = bf16[1,16,8192]{2,1,0:T(8,128)(2,1)} copy(bf16[1,16,8192]{2,1,0:T(8,128)(2,1)} %bitcast.7) | data formatting | bytes 524288

commit v5 on v4

--- a/solution.py
+++ b/solution.py
@@ -23,7 +23,7 @@
     nv_hbm,
     mk_hbm,
     mv_hbm,
-    lists,
+    lists_hbm,
     o_ref,
     q_v,
     mk_v,
@@ -39,6 +39,7 @@
     value_tiles,
     filler,
     table,
+    lists,
     local_sem,
     recv_sem,
     far_sem,
@@ -49,6 +50,7 @@
     prev_sem,
     out_send,
     out_recv,
+    word_sem,
 ):
     mem_count, head_count, span_count, unit_count, list_length, group, scale = sizes
     ring = mem_count // 2
@@ -74,9 +76,11 @@
         pltpu.make_async_copy(mk_hbm, mk_v, local_sem.at[2]),
         pltpu.make_async_copy(mv_hbm, mv_v, local_sem.at[3]),
         pltpu.make_async_copy(q_hbm, q_v, local_sem.at[4]),
+        pltpu.make_async_copy(lists_hbm, lists, local_sem.at[5]),
     ]
     loads[0].start()
     loads[1].start()
+    loads[5].start()
 
     barrier = pltpu.get_barrier_semaphore()
     near = [
@@ -91,15 +95,28 @@
             device_id=device(z + dz, core if dc == 0 else 1 - core, span + dx),
             device_id_type=MESH,
         )
-    for load in loads[2:]:
+    for load in loads[2:5]:
         load.start()
-    for dy in range(1, head_count):
+    beyond = [lax.rem(head + hop, head_count) for hop in (1, head_count - 1)]
+    for head_at in beyond:
         pl.semaphore_signal(
-            barrier,
-            inc=1,
-            device_id=device(z, core, span, lax.rem(head + dy, head_count)),
-            device_id_type=MESH,
-        )
+            barrier, inc=1, device_id=device(z, core, span, head_at), device_id_type=MESH
+        )
+
+    rounds = head_count // 2 - 1
+
+    def tell(turn):
+        for way, head_at in enumerate(beyond):
+            pl.semaphore_signal(
+                word_sem.at[way, turn],
+                inc=1,
+                device_id=device(z, core, span, head_at),
+                device_id_type=MESH,
+            )
+
+    def hear(turn):
+        for way in range(2):
+            pl.semaphore_wait(word_sem.at[way, turn], 1)
 
     def owner(entry):
         return lists[0, entry] // unit_count
@@ -170,6 +187,7 @@
         send_down(mem, item, 0).start()
         send_side(mem, item).start()
 
+    loads[5].wait()
     owners = [owner(entry) for entry in range(list_length)]
     picks = [jnp.int32(0)] * SLOTS
     rank = jnp.int32(0)
@@ -182,7 +200,7 @@
         rank = rank + here.astype(jnp.int32)
     loads[0].wait()
     loads[1].wait()
-    pl.semaphore_wait(barrier, len(near) + head_count - 1)
+    pl.semaphore_wait(barrier, len(near) + 2)
     send_own(0)
     send_prev().start()
     loads[2].wait()
@@ -200,6 +218,8 @@
         ranks.append(same)
     for item in range(1, ITEMS):
         send_own(item)
+    if rounds > 0:
+        tell(0)
     distant = [(held // 2 == far_z).astype(jnp.int32) for held in owners]
     place_far = jnp.int32(list_length) - sum(distant)
     place_near = jnp.int32(0)
@@ -348,6 +368,13 @@
 
         send_side(above, item).start()
 
+        for turn in range(1, rounds):
+
+            @pl.when(tick == turn * ITEMS)
+            def _():
+                hear(turn - 1)
+                tell(turn)
+
         @pl.when(tick == 1)
         def _():
             begin()
@@ -384,6 +411,8 @@
             put_unit(place - first, place, False)
         absorb(past - first)
 
+    if rounds > 0:
+        hear(rounds - 1)
     for item in range(ITEMS):
         far_copy(1 - core, item).wait_recv()
 
@@ -491,7 +520,7 @@
         out_shape=jax.ShapeDtypeStruct(
             (length // head_count, head_count * group * width), jnp.bfloat16
         ),
-        in_specs=[anywhere] * 5 + [pl.BlockSpec(memory_space=pltpu.SMEM)],
+        in_specs=[anywhere] * 6,
         out_specs=anywhere,
         scratch_shapes=[
             pltpu.VMEM((rows, width), jnp.bfloat16),
@@ -508,7 +537,8 @@
             pltpu.VMEM((tiles * unit_length, 2 * width), jnp.bfloat16),
             pltpu.VMEM((unit_length, width), jnp.bfloat16),
             pltpu.SMEM((list_length,), jnp.int32),
-            dma((5,)),
+            pltpu.SMEM((1, list_length), jnp.int32),
+            dma((6,)),
             dma((mem_count, ITEMS)),
             dma((2, ITEMS)),
             dma((ring, ITEMS)),
@@ -518,6 +548,7 @@
             dma((2,)),
             dma((head_count,)),
             dma((head_count,)),
+            pltpu.SemaphoreType.REGULAR((2, max(1, head_count // 2 - 1))),
         ],
         compiler_params=pltpu.CompilerParams(
             collective_id=0, has_side_effects=True, vmem_limit_bytes=62 * 1024 * 1024

time: 52.6 us -> 51.2 us (0.973)
  Pallas kernels: 50.7 us -> 49.3 us
    pallas_call x1, Pallas kernels: 50.7 us -> 49.3 us  [local(): pl.pallas_call(functools.partial(kernel, sizes), out_shape=jax.ShapeDtype...]
where the time goes in v5:
time: 51.2 us; the launch traced here: 51 us
  Pallas kernels  49.3 us (96%)
  local copies, waits for them, and re-layouts  1.67 us (3%)
    pallas_call x1, Pallas kernels, local(): pl.pallas_call(functools.partial(kernel, sizes), out_shape=jax.ShapeDtype...  49.3 us
    unnamed x1, local copies, waits for them, and re-layouts  1.67 us

profile of v5, /device:TPU:1, one launch (start us, length us, event | category | flops | bytes accessed | tf_op | source)
XLA Modules:
  0.0 51.0 jit_solution(1369578355639398113)
XLA Ops:
  0.0 49.3 %shard_map.64 = bf16[16,8192]{1,0:T(8,128)(2,1)} custom-call(bf16[1024,128]{1,0:T(8,128)(2,1)} %bitcast.10, bf16[128,128]{1,0:T(8,128)(2,1)} %bitcast.11, bf16[128,128]{1,0:T(8,128)(2,1)} %bitcast.12, bf16[32,128,128]{2,1,0:T(8,128)(2,1)} %bitcast.8, bf16[32,128,128]{2,1,0:T(8,128)(2,1)} %bitcast.9, s32[1,16]{1,0:T(1,128)} %bitcast.13), custom_call_target="tpu_custom_call" | custom-call | tf_op jit(solution)/shard_map/pallas_call | solution.py:518
  49.4 1.7 %copy.8 = bf16[1,16,8192]{2,1,0:T(8,128)(2,1)} copy(bf16[1,16,8192]{2,1,0:T(8,128)(2,1)} %bitcast.7) | data formatting | bytes 524288

commit v6 on v5

--- a/solution.py
+++ b/solution.py
@@ -391,7 +391,8 @@
                 put_chunk(tile, source, buf[source, 0, 0], buf[source, 1, 0])
             absorb(4)
 
-    early = min(list_length // 2, list_length - 2 * SLOTS)
+    sure = list_length - 2 * SLOTS
+    early = min(3 * list_length // 8, sure) // 2 * 2
     for item in range(1, ITEMS):
         wait_item(beside, item)
 
@@ -402,17 +403,26 @@
         wait_item(at(z - step, 1 - core), item)
         wait_item(at(z + step, 1 - core), item)
 
+    def put_early(first, past):
+        for place in range(first, past):
+            put_unit(place - first, place, False)
+
+    split = min(ITEMS, early)
+    put_early(0, split)
     for half in range(2):
         for item in (half, half + ITEMS // 2):
             far_copy(core, item).wait_recv()
             far_copy(core, item).start()
-        first, past = half * early // 2, (half + 1) * early // 2
-        for place in range(first, past):
-            put_unit(place - first, place, False)
-        absorb(past - first)
+        if half == 0:
+            absorb(split)
+        elif early > split:
+            put_early(split, early)
+            absorb(early - split)
 
     if rounds > 0:
         hear(rounds - 1)
+    for place in range(early, sure):
+        put_unit(2 + place - early, place, False)
     for item in range(ITEMS):
         far_copy(1 - core, item).wait_recv()
 
@@ -435,7 +445,7 @@
 
     for origin in range(2):
         put_chunk(origin, far_z * 2 + origin, far[origin, 0, 0], far[origin, 1, 0])
-    for place in range(early, list_length):
+    for place in range(sure, list_length):
         put_unit(2 + place - early, place, True)
     half = head_count // 2
     hops = [half]

time: 51.2 us -> 51.5 us (level)
  no operation moved by 1% of the time
where the time goes in v6:
time: 51.5 us; the launch traced here: 51.3 us
  Pallas kernels  49.7 us (97%)
  local copies, waits for them, and re-layouts  1.67 us (3%)
    pallas_call x1, Pallas kernels, local(): pl.pallas_call(functools.partial(kernel, sizes), out_shape=jax.ShapeDtype...  49.7 us
    unnamed x1, local copies, waits for them, and re-layouts  1.67 us

profile of v6, /device:TPU:1, one launch (start us, length us, event | category | flops | bytes accessed | tf_op | source)
XLA Modules:
  0.0 51.3 jit_solution(10714809005139618858)
XLA Ops:
  0.0 49.7 %shard_map.64 = bf16[16,8192]{1,0:T(8,128)(2,1)} custom-call(bf16[1024,128]{1,0:T(8,128)(2,1)} %bitcast.10, bf16[128,128]{1,0:T(8,128)(2,1)} %bitcast.11, bf16[128,128]{1,0:T(8,128)(2,1)} %bitcast.12, bf16[32,128,128]{2,1,0:T(8,128)(2,1)} %bitcast.8, bf16[32,128,128]{2,1,0:T(8,128)(2,1)} %bitcast.9, s32[1,16]{1,0:T(1,128)} %bitcast.13), custom_call_target="tpu_custom_call" | custom-call | tf_op jit(solution)/shard_map/pallas_call | solution.py:528
  49.7 1.7 %copy.8 = bf16[1,16,8192]{2,1,0:T(8,128)(2,1)} copy(bf16[1,16,8192]{2,1,0:T(8,128)(2,1)} %bitcast.7) | data formatting | bytes 524288

commit v7 on v6

--- a/solution.py
+++ b/solution.py
@@ -298,7 +298,7 @@
             result = accum[rows, :] * jnp.concatenate([factor, factor], axis=1) + result
         return result
 
-    def attend_all(blocks, width, masks_of, fresh, finish):
+    def attend_all(blocks, width, masks_of, fresh, finish, prompt=False):
         count = len(blocks)
         scores = score(blocks[0], width, masks_of(0))
         weighed = None
@@ -309,7 +309,10 @@
             done = weighed
             if index < count:
                 weighed = weigh(blocks[index], width, scores, fresh)
-            if done is not None:
+            if prompt and index < count:
+                new_peak, factor, weights = weighed
+                finish(index, new_peak, combine(blocks[index], width, weights, factor))
+            elif done is not None and not prompt:
                 new_peak, factor, weights = done
                 finish(index - 1, new_peak, combine(blocks[index - 1], width, weights, factor))
             scores = following
@@ -468,7 +471,7 @@
         else:
             keep_out().start()
 
-    attend_all(parts, (2 + list_length - early) * LANES, lambda turn: {}, False, hand_over)
+    attend_all(parts, (2 + list_length - early) * LANES, lambda turn: {}, False, hand_over, True)
 
     send_prev().wait_send()
 

time: 51.5 us -> 51.5 us (level)
  no operation moved by 1% of the time
where the time goes in v7:
time: 51.5 us; the launch traced here: 51.3 us
  Pallas kernels  49.6 us (96%)
  local copies, waits for them, and re-layouts  1.67 us (3%)
    pallas_call x1, Pallas kernels, local(): pl.pallas_call(functools.partial(kernel, sizes), out_shape=jax.ShapeDtype...  49.6 us
    unnamed x1, local copies, waits for them, and re-layouts  1.67 us

profile of v7, /device:TPU:1, one launch (start us, length us, event | category | flops | bytes accessed | tf_op | source)
XLA Modules:
  0.0 51.3 jit_solution(1717340392406932578)
XLA Ops:
  0.0 49.6 %shard_map.64 = bf16[16,8192]{1,0:T(8,128)(2,1)} custom-call(bf16[1024,128]{1,0:T(8,128)(2,1)} %bitcast.10, bf16[128,128]{1,0:T(8,128)(2,1)} %bitcast.11, bf16[128,128]{1,0:T(8,128)(2,1)} %bitcast.12, bf16[32,128,128]{2,1,0:T(8,128)(2,1)} %bitcast.8, bf16[32,128,128]{2,1,0:T(8,128)(2,1)} %bitcast.9, s32[1,16]{1,0:T(1,128)} %bitcast.13), custom_call_target="tpu_custom_call" | custom-call | tf_op jit(solution)/shard_map/pallas_call | solution.py:531
  49.6 1.7 %copy.8 = bf16[1,16,8192]{2,1,0:T(8,128)(2,1)} copy(bf16[1,16,8192]{2,1,0:T(8,128)(2,1)} %bitcast.7) | data formatting | bytes 524288
